TPU v7x, 32 devices: a whole 2x2x4 slice. The times are simulated.
32 devices in a mesh: seq: 2 (over y), row: 4 (over x, core), rep: 4 (over z).
Axes of the slice: x: 2, y: 2, z: 4, core: 2. Of those that a mesh axis runs over, the one named last changes fastest.
Arguments:
- block_input: bfloat16 [4, 2048, 2048], P('row', 'seq', 'rep'), may hold values from -6 to 6
- cotangent: bfloat16 [4, 2048, 2048], P('row', 'seq', 'rep'), may hold values from -6 to 6
- segment_ids: int32 [4, 2048], P('row', 'seq'), may hold values from 0 to 3, never falling along the last dimension, each value on 1 to 1024 neighbouring positions
- pad_mask: int32 [4, 2048], P('row', 'seq'), may hold values 0 or 1
- state_init: float32 [4, 2816], P('row', 'rep'), may hold values from -6 to 6
- window_init: bfloat16 [4, 3, 2816], P('row', None, 'rep'), may hold values from -6 to 6
- recur_input: bfloat16 [2048, 2816], P(('seq', 'row'), 'rep'), may hold values from -0.125 to 0.125
- recur_gate: bfloat16 [2048, 2816], P(('seq', 'row'), 'rep'), may hold values from -0.125 to 0.125
- recur_output: bfloat16 [2048, 2816], P(('seq', 'row'), 'rep'), may hold values from -0.3125 to 0.3125
- feed_gate: bfloat16 [2048, 6144], P(('seq', 'row'), 'rep'), may hold values from -0.125 to 0.125
- feed_up: bfloat16 [2048, 6144], P(('seq', 'row'), 'rep'), may hold values from -0.125 to 0.125
- feed_down: bfloat16 [2048, 6144], P(('seq', 'row'), 'rep'), may hold values from -0.15625 to 0.15625
- conv_kernel: float32 [4, 2816], P(None, 'rep'), may hold values from -3 to 3
- conv_bias: float32 [2816], P('rep'), may hold values from -3 to 3
- decay_gate: bfloat16 [16, 176, 176], P('rep'), may hold values from -0.4375 to 0.4375
- input_gate: bfloat16 [16, 176, 176], P('rep'), may hold values from -0.4375 to 0.4375
- decay_bias: float32 [2816], P('rep'), may hold values from -4 to 4
- input_bias: float32 [2816], P('rep'), may hold values from -4 to 4
- decay_logit: float32 [2816], P('rep'), may hold values from -10.5 to -4.5
- mixer_gain: float32 [2048], replicated, may hold values from 0.25 to 1.75
- feed_gain: float32 [2048], replicated, may hold values from 0.25 to 1.75
Outputs:
- block_output: bfloat16 [4, 2048, 2048], P('row', 'seq', 'rep')
- block_states: float32 [4, 2, 2816], P('row', 'seq', 'rep')
- block_windows: bfloat16 [4, 2, 3, 2816], P('row', 'seq', None, 'rep')
- input_grad: bfloat16 [4, 2048, 2048], P('row', 'seq', 'rep')
- recur_input_grad: float32 [2048, 2816], P(('seq', 'row'), 'rep')
- recur_gate_grad: float32 [2048, 2816], P(('seq', 'row'), 'rep')
- recur_output_grad: float32 [2048, 2816], P(('seq', 'row'), 'rep')
- feed_gate_grad: float32 [2048, 6144], P(('seq', 'row'), 'rep')
- feed_up_grad: float32 [2048, 6144], P(('seq', 'row'), 'rep')
- feed_down_grad: float32 [2048, 6144], P(('seq', 'row'), 'rep')
- conv_kernel_grad: float32 [4, 2816], P(None, 'rep')
- conv_bias_grad: float32 [2816], P('rep')
- decay_gate_grad: float32 [16, 176, 176], P('rep')
- input_gate_grad: float32 [16, 176, 176], P('rep')
- decay_bias_grad: float32 [2816], P('rep')
- input_bias_grad: float32 [2816], P('rep')
- decay_logit_grad: float32 [2816], P('rep')
- mixer_gain_grad: float32 [2048], replicated
- feed_gain_grad: float32 [2048], replicated
Inputs may be any that keep to these rules, and one draw needn't show every extreme that they name: `segment_ids`: document numbers never fall along a row; each row holds 4 documents of at most 1024 positions.
All inputs are finite; a program needn't handle non-finite values. No bound on the sum of `pad_mask` on one device may be relied on, other than what follows from the above.
Results may differ from a plain program's by a relative error of at most 0.01.
Values may be sent and summed in bfloat16 or wider, within the bound.
A program may use at most 384 MiB of HBM per device.

v0:
```python
from functools import partial
import jax
import jax.numpy as jnp
from jax import lax
from jax.sharding import PartitionSpec as P

eps = 1e-06


def shifted_2(block, axis, distance):
    devices = range(lax.axis_size(axis))
    route = [(i - distance, i) for i in devices if i - distance in devices]
    return lax.ppermute(block, axis, route)


def entering(value, axis, join, neutral, backward):
    count, mine = (lax.axis_size(axis), lax.axis_index(axis))
    pieces = jax.tree.map(lambda part: lax.all_gather(part, axis), value)
    if backward:
        pieces = jax.tree.map(lambda part: part[::-1], pieces)
        mine = count - 1 - mine
    subtotal = jax.tree.map(
        lambda part, zero: jnp.full_like(part, 0) + jnp.asarray(zero, part.dtype), value, neutral
    )

    def hop(position, subtotal):
        longer = join(subtotal, jax.tree.map(lambda part: part[position], pieces))
        return jax.tree.map(lambda new, old: jnp.where(position < mine, new, old), longer, subtotal)

    return lax.fori_loop(0, count - 1, hop, subtotal)


def rms_norm(values, scales):
    return values * lax.rsqrt(jnp.mean(values * values, axis=-1, keepdims=True) + eps) * scales


def affine(former, latter):
    return (former[0] * latter[0], latter[0] * former[1] + latter[1])


def conv_math(padded, kernel, offset_bias, same_masks):
    tap_count = kernel.shape[0]
    length = padded.shape[1] - tap_count + 1
    total = offset_bias
    for offset in range(tap_count):
        start = tap_count - 1 - offset
        total = (
            total
            + kernel[offset] * padded[:, start : start + length] * same_masks[offset][..., None]
        )
    return total


def gate_math(conv_out, decay_pre, input_pre, decay_logit, retain_mask):
    rate_scale = 8.0 * jax.nn.softplus(decay_logit)
    exponent = rate_scale * jax.nn.sigmoid(decay_pre)
    retain = retain_mask[..., None] * jnp.exp(-exponent)
    inflow = jnp.sqrt(-jnp.expm1(-2.0 * exponent)) * jax.nn.sigmoid(input_pre) * conv_out
    return (retain, inflow)


def output_gate(hidden, gate_branch):
    return hidden * jax.nn.gelu(gate_branch, approximate=True)


def feed_math(gate_pre, up_pre):
    return jax.nn.gelu(gate_pre, approximate=True) * up_pre


def contract_last(left, right):
    return lax.dot_general(
        left, right, (((2,), (1,)), ((), ())), preferred_element_type=jnp.float32
    )


def outer_sum(left, right):
    return jnp.einsum("rtd,rtm->dm", left, right, preferred_element_type=jnp.float32)


def split_heads(values, head_count):
    return values.reshape(
        values.shape[0], values.shape[1], head_count, values.shape[2] // head_count
    )


def block_apply(values, blocks):
    row_count, length, channels = values.shape
    heads_in = split_heads(values, blocks.shape[0])
    mixed = jnp.einsum("rthi,hij->rthj", heads_in, blocks, preferred_element_type=jnp.float32)
    return mixed.reshape(row_count, length, channels)


def block_apply_back(grads, blocks):
    row_count, length, channels = grads.shape
    heads_in = split_heads(grads, blocks.shape[0])
    mixed = jnp.einsum("rthj,hij->rthi", heads_in, blocks, preferred_element_type=jnp.float32)
    return mixed.reshape(row_count, length, channels)


def block_outer(values, grads, head_count):
    return jnp.einsum(
        "rthi,rthj->hij",
        split_heads(values, head_count),
        split_heads(grads, head_count),
        preferred_element_type=jnp.float32,
    )


def shards(
    block_input,
    cotangent,
    segment_ids,
    pad_mask,
    state_init,
    window_init,
    recur_input,
    recur_gate,
    recur_output,
    feed_gate,
    feed_up,
    feed_down,
    conv_kernel,
    conv_bias,
    decay_gate,
    input_gate,
    decay_bias,
    input_bias,
    decay_logit,
    mixer_gain,
    feed_gain,
):
    own_width = block_input.shape[2]
    rep_index = lax.axis_index("rep")
    at_start = lax.axis_index("seq") == 0
    head_count = decay_gate.shape[0]
    tap_count = conv_kernel.shape[0]
    edge_width = tap_count - 1
    length = segment_ids.shape[1]
    masked_low = cotangent * pad_mask[..., None].astype(jnp.bfloat16)
    whole_input, whole_masked = (
        lax.all_gather(block_input, "rep", axis=2, tiled=True),
        lax.all_gather(masked_low, "rep", axis=2, tiled=True),
    )
    fetched = (
        lax.all_gather(recur_input, ("seq", "row"), axis=0, tiled=True),
        lax.all_gather(recur_gate, ("seq", "row"), axis=0, tiled=True),
        lax.all_gather(recur_output, ("seq", "row"), axis=0, tiled=True),
        lax.all_gather(feed_gate, ("seq", "row"), axis=0, tiled=True),
        lax.all_gather(feed_up, ("seq", "row"), axis=0, tiled=True),
        lax.all_gather(feed_down, ("seq", "row"), axis=0, tiled=True),
    )
    input_float = whole_input.astype(jnp.float32)
    normed_f, norm_one_back = jax.vjp(rms_norm, input_float, mixer_gain)
    normed = normed_f.astype(jnp.bfloat16)
    conv_input = jnp.dot(normed, fetched[0], preferred_element_type=jnp.float32).astype(
        jnp.bfloat16
    )
    gate_branch = jnp.dot(normed, fetched[1], preferred_element_type=jnp.float32)
    left_input, left_marks = shifted_2(
        (conv_input[:, -edge_width:], segment_ids[:, -edge_width:].astype(jnp.bfloat16)), "seq", 1
    )
    left_ids = left_marks.astype(jnp.int32)
    left_ids = jnp.where(at_start, jnp.broadcast_to(segment_ids[:, :1], left_ids.shape), left_ids)
    left_input = jnp.where(at_start, window_init, left_input)
    ids_ext = jnp.concatenate([left_ids, segment_ids], axis=1)
    same_masks = [
        (ids_ext[:, edge_width - offset : edge_width - offset + length] == segment_ids).astype(
            jnp.float32
        )
        for offset in range(tap_count)
    ]
    retain_mask = (ids_ext[:, edge_width - 1 : edge_width - 1 + length] == segment_ids).astype(
        jnp.float32
    )
    padded = jnp.concatenate([left_input, conv_input], axis=1).astype(jnp.float32)
    conv_out, conv_back = jax.vjp(
        partial(conv_math, same_masks=same_masks), padded, conv_kernel, conv_bias
    )
    conv_low = conv_out.astype(jnp.bfloat16)
    decay_pre = block_apply(conv_low, decay_gate) + decay_bias
    input_pre = block_apply(conv_low, input_gate) + input_bias
    (retain, inflow), gate_back = jax.vjp(
        partial(gate_math, retain_mask=retain_mask), conv_out, decay_pre, input_pre, decay_logit
    )
    products, partial_states = lax.associative_scan(affine, (retain, inflow), axis=1)
    carry_decay, carry_state = entering(
        (products[:, -1], partial_states[:, -1]),
        "seq",
        affine,
        (jnp.ones_like(state_init), jnp.zeros_like(state_init)),
        False,
    )
    state_in = carry_decay * state_init + carry_state
    hidden = partial_states + products * state_in[:, None]
    block_states = hidden[:, -1:]
    block_windows = conv_input[:, None, -edge_width:]
    gated_f, gated_back = jax.vjp(output_gate, hidden, gate_branch)
    gated = gated_f.astype(jnp.bfloat16)
    branch = lax.psum(contract_last(gated, fetched[2]), "rep")
    middle = input_float + branch
    normed_mid_f, norm_two_back = jax.vjp(rms_norm, middle, feed_gain)
    normed_mid = normed_mid_f.astype(jnp.bfloat16)
    gate_pre = jnp.dot(normed_mid, fetched[3], preferred_element_type=jnp.float32)
    up_pre = jnp.dot(normed_mid, fetched[4], preferred_element_type=jnp.float32)
    feed_f, feed_back = jax.vjp(feed_math, gate_pre, up_pre)
    feed_low = feed_f.astype(jnp.bfloat16)
    feed_out = lax.psum_scatter(
        contract_last(feed_low, fetched[5]), "rep", scatter_dimension=2, tiled=True
    )
    middle_own = lax.dynamic_slice_in_dim(middle, rep_index * own_width, own_width, 2)
    block_output = (middle_own + feed_out).astype(jnp.bfloat16)
    back_weights = (
        lax.all_gather(recur_input, ("seq", "row"), axis=0, tiled=True),
        lax.all_gather(recur_gate, ("seq", "row"), axis=0, tiled=True),
        lax.all_gather(recur_output, ("seq", "row"), axis=0, tiled=True),
        lax.all_gather(feed_gate, ("seq", "row"), axis=0, tiled=True),
        lax.all_gather(feed_up, ("seq", "row"), axis=0, tiled=True),
        lax.all_gather(feed_down, ("seq", "row"), axis=0, tiled=True),
    )
    grad_feed = jnp.dot(whole_masked, back_weights[5], preferred_element_type=jnp.float32)
    feed_down_grad = outer_sum(whole_masked, feed_low)
    gate_grad_f, up_grad_f = feed_back(grad_feed)
    gate_grad = gate_grad_f.astype(jnp.bfloat16)
    up_grad = up_grad_f.astype(jnp.bfloat16)
    feed_gate_grad = outer_sum(normed_mid, gate_grad)
    feed_up_grad = outer_sum(normed_mid, up_grad)
    mid_normed_grad = lax.psum(
        contract_last(gate_grad, back_weights[3]) + contract_last(up_grad, back_weights[4]), "rep"
    )
    middle_norm_grad, feed_gain_grad = norm_two_back(mid_normed_grad)
    middle_grad = whole_masked.astype(jnp.float32) + middle_norm_grad
    middle_low = middle_grad.astype(jnp.bfloat16)
    gated_grad = jnp.dot(middle_low, back_weights[2], preferred_element_type=jnp.float32)
    recur_output_grad = outer_sum(middle_low, gated)
    hidden_grad, branch_grad_f = gated_back(gated_grad)
    branch_grad = branch_grad_f.astype(jnp.bfloat16)
    shifted = jnp.concatenate([retain[:, 1:], jnp.ones_like(retain[:, :1])], axis=1)
    after_decay, local_adjoint = lax.associative_scan(
        affine, (shifted, hidden_grad), axis=1, reverse=True
    )
    carry_back = entering(
        (products[:, -1], retain[:, 0] * local_adjoint[:, 0]),
        "seq",
        affine,
        (jnp.ones_like(state_init), jnp.zeros_like(state_init)),
        True,
    )
    adjoint = local_adjoint + after_decay * carry_back[1][:, None]
    hidden_prev = jnp.concatenate([state_in[:, None], hidden[:, :-1]], axis=1)
    conv_direct, decay_pre_f, input_pre_f, decay_logit_grad = gate_back(
        (adjoint * hidden_prev, adjoint)
    )
    decay_pre_grad = decay_pre_f.astype(jnp.bfloat16)
    input_pre_grad = input_pre_f.astype(jnp.bfloat16)
    decay_gate_grad = block_outer(conv_low, decay_pre_grad, head_count)
    input_gate_grad = block_outer(conv_low, input_pre_grad, head_count)
    decay_bias_grad = jnp.sum(decay_pre_grad.astype(jnp.float32), axis=(0, 1))
    input_bias_grad = jnp.sum(input_pre_grad.astype(jnp.float32), axis=(0, 1))
    conv_grad = (
        conv_direct
        + block_apply_back(decay_pre_grad, decay_gate)
        + block_apply_back(input_pre_grad, input_gate)
    )
    padded_grad, conv_kernel_grad, conv_bias_grad = conv_back(conv_grad)
    from_right = shifted_2(padded_grad[:, :edge_width], "seq", -1)
    own_grad = padded_grad[:, edge_width:]
    own_grad = jnp.concatenate(
        [own_grad[:, :-edge_width], own_grad[:, -edge_width:] + from_right], axis=1
    )
    input_low_grad = own_grad.astype(jnp.bfloat16)
    recur_input_grad = outer_sum(normed, input_low_grad)
    recur_gate_grad = outer_sum(normed, branch_grad)
    normed_terms = contract_last(input_low_grad, back_weights[0]) + contract_last(
        branch_grad, back_weights[1]
    )
    middle_grad_own = lax.dynamic_slice_in_dim(middle_grad, rep_index * own_width, own_width, 2)
    normed_grad = lax.psum(normed_terms, "rep")
    input_norm_grad, mixer_gain_grad = norm_one_back(normed_grad)
    input_norm_own = lax.dynamic_slice_in_dim(input_norm_grad, rep_index * own_width, own_width, 2)
    input_grad = (middle_grad_own + input_norm_own).astype(jnp.bfloat16)
    matrix_grads = (
        lax.psum_scatter(recur_input_grad, ("seq", "row"), scatter_dimension=0, tiled=True),
        lax.psum_scatter(recur_gate_grad, ("seq", "row"), scatter_dimension=0, tiled=True),
        lax.psum_scatter(recur_output_grad, ("seq", "row"), scatter_dimension=0, tiled=True),
        lax.psum_scatter(feed_gate_grad, ("seq", "row"), scatter_dimension=0, tiled=True),
        lax.psum_scatter(feed_up_grad, ("seq", "row"), scatter_dimension=0, tiled=True),
        lax.psum_scatter(feed_down_grad, ("seq", "row"), scatter_dimension=0, tiled=True),
    )
    small_grads = lax.psum(
        (
            conv_kernel_grad,
            conv_bias_grad,
            decay_gate_grad,
            input_gate_grad,
            decay_bias_grad,
            input_bias_grad,
            decay_logit_grad,
            mixer_gain_grad,
            feed_gain_grad,
        ),
        ("seq", "row"),
    )
    return (
        block_output,
        block_states,
        block_windows,
        input_grad,
        matrix_grads[0],
        matrix_grads[1],
        matrix_grads[2],
        matrix_grads[3],
        matrix_grads[4],
        matrix_grads[5],
        small_grads[0],
        small_grads[1],
        small_grads[2],
        small_grads[3],
        small_grads[4],
        small_grads[5],
        small_grads[6],
        small_grads[7],
        small_grads[8],
    )


def solution(mesh):
    in_specs = (
        P("row", "seq", "rep"),
        P("row", "seq", "rep"),
        P("row", "seq"),
        P("row", "seq"),
        P("row", "rep"),
        P("row", None, "rep"),
        P(("seq", "row"), "rep"),
        P(("seq", "row"), "rep"),
        P(("seq", "row"), "rep"),
        P(("seq", "row"), "rep"),
        P(("seq", "row"), "rep"),
        P(("seq", "row"), "rep"),
        P(None, "rep"),
        P("rep"),
        P("rep", None, None),
        P("rep", None, None),
        P("rep"),
        P("rep"),
        P("rep"),
        P(),
        P(),
    )
    out_specs = (
        P("row", "seq", "rep"),
        P("row", "seq", "rep"),
        P("row", "seq", None, "rep"),
        P("row", "seq", "rep"),
        P(("seq", "row"), "rep"),
        P(("seq", "row"), "rep"),
        P(("seq", "row"), "rep"),
        P(("seq", "row"), "rep"),
        P(("seq", "row"), "rep"),
        P(("seq", "row"), "rep"),
        P(None, "rep"),
        P("rep"),
        P("rep", None, None),
        P("rep", None, None),
        P("rep"),
        P("rep"),
        P("rep"),
        P(),
        P(),
    )
    return jax.shard_map(shards, mesh=mesh, in_specs=in_specs, out_specs=out_specs, check_vma=False)
```

profile of v0, /device:TPU:0, one launch (start us, length us, event | category | flops | bytes accessed | tf_op | source)
XLA Modules:
  0.0 4679.4 jit_solution(15603391600166171410)
XLA Ops:
  20.5 72.6 %all-gather.9.cloned.1.call-done = bf16[1,1024,2048]{2,1,0:T(8,128)(2,1)} async-done(((bf16[1,1024,512]{2,1,0:T(8,128)(2,1)}), bf16[1,1024,2048]{2,1,0:T(8,128)(2,1)}) %all-gather.9.cloned.1.call-update) | async-done | bytes 4194320 | tf_op jit(solution)/shard_map/all_gather | solution.py:141
  96.2 29.0 all-gather.11.cloned.1.call-done
  135.3 27.0 all-gather.13.cloned.1.call-done
  181.9 50.8 %slice.699 = f32[1,512,704]{1,2,0:T(8,128)} slice(f32[1,1024,704]{1,2,0:T(8,128)S(1)} %get-tuple-element.180), slice={[0:1:1], [1:1024:2], [0:704:1]} | slice | bytes 2883584 | tf_op jit(solution)/shard_map/slice | solution.py:185
  232.7 50.7 %slice.703 = f32[1,512,704]{1,2,0:T(8,128)} slice(f32[1,1024,704]{1,2,0:T(8,128)S(1)} %get-tuple-element.180), slice={[0:1:1], [0:1023:2], [0:704:1]} | slice | bytes 2883584 | tf_op jit(solution)/shard_map/slice | solution.py:185
  283.5 51.4 %slice.700 = f32[1,512,704]{1,2,0:T(8,128)} slice(f32[1,1024,704]{1,2,0:T(8,128)} %get-tuple-element.181), slice={[0:1:1], [0:1023:2], [0:704:1]} | slice | bytes 2883584 | tf_op jit(solution)/shard_map/slice | solution.py:185
  334.9 51.3 %slice.701 = f32[1,512,704]{1,2,0:T(8,128)} slice(f32[1,1024,704]{1,2,0:T(8,128)} %get-tuple-element.181), slice={[0:1:1], [1:1024:2], [0:704:1]} | slice | bytes 2883584 | tf_op jit(solution)/shard_map/slice | solution.py:185
  391.1 28.3 slice.706
  419.4 28.3 slice.707
  447.7 28.5 slice.705
  476.2 28.3 slice.709
  541.2 17.2 slice.711
  795.7 28.2 slice.704
  823.9 28.6 slice.769
  856.0 50.7 %slice.698 = f32[1,511,704]{1,2,0:T(8,128)} slice(f32[1,1024,704]{1,2,0:T(8,128)S(1)} %get-tuple-element.180), slice={[0:1:1], [2:1024:2], [0:704:1]} | slice | bytes 2877952 | tf_op jit(solution)/shard_map/slice | solution.py:185
  906.7 51.2 %slice.771 = f32[1,511,704]{1,2,0:T(8,128)} slice(f32[1,1024,704]{1,2,0:T(8,128)} %get-tuple-element.181), slice={[0:1:1], [2:1024:2], [0:704:1]} | slice | bytes 2877952 | tf_op jit(solution)/shard_map/slice | solution.py:185
  1199.9 28.7 pad.306
  1228.6 28.9 pad.307
  1257.5 28.7 pad.287
  1288.5 28.6 pad.286
  1326.9 57.3 %pad.308 = f32[1,1024,704]{1,2,0:T(8,128)} pad(f32[1,512,704]{1,2,0:T(8,128)} %pad_maximum_fusion.1, f32[]{:T(128)} %constant.20.clone.1), padding=0_0_0x0_1_1x0_0_0 | pad | bytes 4325380 | tf_op jit(solution)/shard_map/pad | solution.py:185
  1384.2 57.2 %pad.309 = f32[1,1024,704]{1,2,0:T(8,128)} pad(f32[1,512,704]{1,2,0:T(8,128)} %add.770, f32[]{:T(128)} %constant.20.clone.1), padding=0_0_0x1_0_1x0_0_0 | pad | bytes 4325380 | tf_op jit(solution)/shard_map/pad | solution.py:185
  1447.5 57.1 %pad.288 = f32[1,1024,704]{1,2,0:T(8,128)} pad(f32[1,512,704]{1,2,0:T(8,128)} %pad_maximum_fusion, f32[]{:T(128)} %constant.20.clone.1), padding=0_0_0x0_1_1x0_0_0 | pad | bytes 4325380 | tf_op jit(solution)/shard_map/pad | solution.py:185
  1504.6 57.3 %pad.289 = f32[1,1024,704]{1,2,0:T(8,128)} pad(f32[1,512,704]{1,2,0:T(8,128)} %add.759, f32[]{:T(128)} %constant.20.clone.1), padding=0_0_0x1_0_1x0_0_0 | pad | bytes 4325380 | tf_op jit(solution)/shard_map/pad | solution.py:185
  1595.3 286.3 %all-reduce.97.cloned.1.call-done = f32[1,1024,2048]{2,1,0:T(8,128)} async-done(((f32[1,1024,2048]{2,1,0:T(8,128)}), f32[1,1024,2048]{2,1,0:T(8,128)}) %all-reduce.97.cloned.1.call-update) | async-done | bytes 8388624 | tf_op jit(solution)/shard_map/psum | solution.py:199
  1893.8 34.1 all-gather.17.cloned.1.call-done
  1939.8 35.6 all-gather.19.cloned.1.call-done
  1987.1 71.2 %all-gather.23.cloned.1.call-done = bf16[1,1024,2048]{2,1,0:T(8,128)(2,1)} async-done(((bf16[1,1024,512]{2,1,0:T(8,128)(2,1)}), bf16[1,1024,2048]{2,1,0:T(8,128)(2,1)}) %all-gather.23.cloned.1.call-update) | async-done | bytes 4194320 | tf_op jit(solution)/shard_map/all_gather | solution.py:142
  2058.3 46.0 all-gather.21.cloned.1.call-done
  2104.3 18.4 multiply_convert_fusion.2
  2146.4 51.2 %slice.798 = f32[1,512,704]{1,2,0:T(8,128)} slice(f32[1,1024,704]{1,2,0:T(8,128)} %concatenate.160), slice={[0:1:1], [0:1023:2], [0:704:1]} | slice | bytes 2883584 | tf_op jit(solution)/shard_map/slice | solution.py:238
  2197.7 51.3 %slice.805 = f32[1,512,704]{1,2,0:T(8,128)} slice(f32[1,1024,704]{1,2,0:T(8,128)} %concatenate.160), slice={[0:1:1], [1:1024:2], [0:704:1]} | slice | bytes 2883584 | tf_op jit(solution)/shard_map/slice | solution.py:238
  2249.0 51.3 %slice.796 = f32[1,511,704]{1,2,0:T(8,128)} slice(f32[1,1024,704]{1,2,0:T(8,128)} %concatenate.160), slice={[0:1:1], [1:1022:2], [0:704:1]} | slice | bytes 2877952 | tf_op jit(solution)/shard_map/slice | solution.py:238
  2352.8 81.8 %all-reduce.99.cloned.1.call-done = f32[1,1024,2048]{2,1,0:T(8,128)} async-done(((f32[1,1024,2048]{2,1,0:T(8,128)}), f32[1,1024,2048]{2,1,0:T(8,128)}) %all-reduce.99.cloned.1.call-update) | async-done | bytes 8388624 | tf_op jit(solution)/shard_map/psum | solution.py:227
  2462.4 51.3 %slice.800 = f32[1,512,704]{1,2,0:T(8,128)} slice(f32[1,1024,704]{1,2,0:T(8,128)} %multiply_bitcast_fusion), slice={[0:1:1], [1:1024:2], [0:704:1]} | slice | bytes 2883584 | tf_op jit(solution)/shard_map/slice | solution.py:238
  2513.7 51.4 %slice.802 = f32[1,512,704]{1,2,0:T(8,128)} slice(f32[1,1024,704]{1,2,0:T(8,128)} %multiply_bitcast_fusion), slice={[0:1:1], [0:1023:2], [0:704:1]} | slice | bytes 2883584 | tf_op jit(solution)/shard_map/slice | solution.py:238
  2596.6 28.3 slice.809
  2624.9 28.3 slice.810
  2653.2 28.3 slice.808
  2681.6 28.7 slice.812
  2763.8 17.0 slice.818
  2959.7 17.1 slice.813
  2997.0 28.2 slice.807
  3025.2 28.4 slice.872
  3057.2 51.3 %slice.874 = f32[1,511,704]{1,2,0:T(8,128)} slice(f32[1,1024,704]{1,2,0:T(8,128)} %multiply_bitcast_fusion), slice={[0:1:1], [1:1022:2], [0:704:1]} | slice | bytes 2877952 | tf_op jit(solution)/shard_map/slice | solution.py:238
  3355.0 28.7 pad.326
  3383.7 28.8 pad.327
  3415.7 57.2 %pad.329 = f32[1,1024,704]{1,2,0:T(8,128)} pad(f32[1,512,704]{1,2,0:T(8,128)} %add.812, f32[]{:T(128)} %constant.20.clone.1), padding=0_0_0x1_0_1x0_0_0 | pad | bytes 4325380 | tf_op jit(solution)/shard_map/pad | solution.py:238
  3475.1 28.6 pad.346
  3503.8 28.9 pad.347
  3554.7 57.2 %pad.328 = f32[1,1024,704]{1,2,0:T(8,128)} pad(f32[1,512,704]{1,2,0:T(8,128)} %pad_maximum_fusion.2, f32[]{:T(128)} %constant.20.clone.1), padding=0_0_0x0_1_1x0_0_0 | pad | bytes 4325380 | tf_op jit(solution)/shard_map/pad | solution.py:238
  3620.2 52.7 %pad.349 = f32[1,1024,704]{1,2,0:T(8,128)S(1)} pad(f32[1,512,704]{1,2,0:T(8,128)} %add.823, f32[]{:T(128)} %constant.20.clone.1), padding=0_0_0x1_0_1x0_0_0 | pad | bytes 4325380 | tf_op jit(solution)/shard_map/pad | solution.py:238
  3676.0 57.2 %pad.348 = f32[1,1024,704]{1,2,0:T(8,128)} pad(f32[1,512,704]{1,2,0:T(8,128)} %concatenate.178, f32[]{:T(128)} %constant.20.clone.1), padding=0_0_0x0_1_1x0_0_0 | pad | bytes 4325380 | tf_op jit(solution)/shard_map/pad | solution.py:238
  3737.2 25.7 rev.5
  3762.9 25.9 rev.4
  3924.4 204.8 %all-reduce.101.cloned.1.call-done = f32[1,1024,2048]{2,1,0:T(8,128)} async-done(((f32[1,1024,2048]{2,1,0:T(8,128)}), f32[1,1024,2048]{2,1,0:T(8,128)}) %all-reduce.101.cloned.1.call-update) | async-done | bytes 8388624 | tf_op jit(solution)/shard_map/psum | solution.py:277
  4137.4 25.4 all-reduce.90
  4167.2 23.5 all-reduce.103.cloned.1.call-done
  4190.7 62.5 %reduce-scatter.14.cloned.1.call-done = f32[256,704]{0,1:T(8,128)} async-done(((f32[2048,704]{0,1:T(8,128)}), f32[256,704]{0,1:T(8,128)}) %reduce-scatter.14.cloned.1.call-update) | async-done | bytes 720912 | tf_op jit(solution)/shard_map/reduce_scatter | solution.py:284
  4253.2 62.9 %reduce-scatter.12.cloned.1.call-done = f32[256,704]{0,1:T(8,128)} async-done(((f32[2048,704]{0,1:T(8,128)}), f32[256,704]{0,1:T(8,128)}) %reduce-scatter.12.cloned.1.call-update) | async-done | bytes 720912 | tf_op jit(solution)/shard_map/reduce_scatter | solution.py:283
  4316.2 63.3 %reduce-scatter.10.cloned.1.call-done = f32[256,704]{0,1:T(8,128)} async-done(((f32[2048,704]{0,1:T(8,128)}), f32[256,704]{0,1:T(8,128)}) %reduce-scatter.10.cloned.1.call-update) | async-done | bytes 720912 | tf_op jit(solution)/shard_map/reduce_scatter | solution.py:282
  4379.5 96.3 %reduce-scatter.16.cloned.1.call-done = f32[256,1536]{1,0:T(8,128)} async-done(((f32[2048,1536]{1,0:T(8,128)}), f32[256,1536]{1,0:T(8,128)}) %reduce-scatter.16.cloned.1.call-update) | async-done | bytes 1572880 | tf_op jit(solution)/shard_map/reduce_scatter | solution.py:285
  4475.8 96.4 %reduce-scatter.18.cloned.1.call-done = f32[256,1536]{1,0:T(8,128)} async-done(((f32[2048,1536]{1,0:T(8,128)}), f32[256,1536]{1,0:T(8,128)}) %reduce-scatter.18.cloned.1.call-update) | async-done | bytes 1572880 | tf_op jit(solution)/shard_map/reduce_scatter | solution.py:286
  4572.2 96.5 %reduce-scatter.20.cloned.1.call-done = f32[256,1536]{1,0:T(8,128)} async-done(((f32[2048,1536]{1,0:T(8,128)}), f32[256,1536]{1,0:T(8,128)}) %reduce-scatter.20.cloned.1.call-update) | async-done | bytes 1572880 | tf_op jit(solution)/shard_map/reduce_scatter | solution.py:287
  (642 shorter events, 1489.7 us)
Async XLA Ops:
  7.2 167.8 %copy-start = (bf16[4,176,176]{2,1,0:T(8,128)(2,1)S(1)}, bf16[4,176,176]{2,1,0:T(8,128)(2,1)}, u32[]{:S(2)}) copy-start(bf16[4,176,176]{2,1,0:T(8,128)(2,1)} %param.36) | copy-start | bytes 743428
  7.2 85.9 %all-gather.9.cloned.1.call-start = ((), (), s32[]{:S(2)}) async-start(), calls=%async_computation.7 | async-start | bytes 5242880 | tf_op jit(solution)/shard_map/all_gather | solution.py:141
  7.9 117.3 %copy-start.98 = (f32[2048]{0:T(1024)S(1)}, f32[2048]{0:T(1024)}, u32[]{:S(2)}) copy-start(f32[2048]{0:T(1024)} %param.40) | copy-start | bytes 24580
  8.0 117.3 %all-gather.11.cloned.1.call-start = ((), (), s32[]{:S(2)}) async-start(), calls=%async_computation.8 | async-start | bytes 3244032 | tf_op jit(solution)/shard_map/all_gather | solution.py:145
  8.7 153.6 %all-gather.13.cloned.1.call-start = ((), (), s32[]{:S(2)}) async-start(), calls=%async_computation.9 | async-start | bytes 3244032 | tf_op jit(solution)/shard_map/all_gather | solution.py:146
  9.4 1572.1 %all-gather.15.cloned.1.call-start = ((), (), s32[]{:S(2)}) async-start(), calls=%async_computation.10 | async-start | bytes 3244032 | tf_op jit(solution)/shard_map/all_gather | solution.py:147
  10.2 8.6 collective-permute-start.1
  15.1 1866.5 %all-reduce.97.cloned.1.call-start = ((), (), s32[]{:S(2)}) async-start(), calls=%async_computation.11 | async-start | bytes 16777216 | tf_op jit(solution)/shard_map/psum | solution.py:199
  18.1 153.1 %copy-start.84 = (f32[704]{0:T(1024)}, f32[704]{0:T(1024)S(1)}, u32[]{:S(2)}) copy-start(f32[704]{0:T(1024)S(1)} %get-tuple-element.143) | copy-start | bytes 8452
  18.1 153.1 %copy-start.86 = (f32[704]{0:T(1024)}, f32[704]{0:T(1024)S(1)}, u32[]{:S(2)}) copy-start(f32[704]{0:T(1024)S(1)} %get-tuple-element.144) | copy-start | bytes 8452
  18.1 153.1 %copy-start.88 = (f32[704]{0:T(1024)}, f32[704]{0:T(1024)S(1)}, u32[]{:S(2)}) copy-start(f32[704]{0:T(1024)S(1)} %get-tuple-element.145) | copy-start | bytes 8452
  18.1 153.0 %copy-start.90 = (f32[704]{0:T(1024)}, f32[704]{0:T(1024)S(1)}, u32[]{:S(2)}) copy-start(f32[704]{0:T(1024)S(1)} %get-tuple-element.146) | copy-start | bytes 8452
  18.8 158.0 %copy-start.71 = (f32[704]{0:T(1024)}, f32[704]{0:T(1024)S(1)}, u32[]{:S(2)}) copy-start(f32[704]{0:T(1024)S(1)} %fusion.79) | copy-start | bytes 8452
  20.5 150.7 %copy-start.78 = (f32[1,1024]{1,0:T(1,128)}, f32[1,1024]{1,0:T(1,128)S(1)}, u32[]{:S(2)}) copy-start(f32[1,1024]{1,0:T(1,128)S(1)} %get-tuple-element.273) | copy-start | bytes 12292
  20.5 150.7 %copy-start.80 = (f32[1,1024]{1,0:T(1,128)}, f32[1,1024]{1,0:T(1,128)S(1)}, u32[]{:S(2)}) copy-start(f32[1,1024]{1,0:T(1,128)S(1)} %get-tuple-element.274) | copy-start | bytes 12292
  20.5 156.4 %copy-start.69 = (f32[1,1024]{1,0:T(1,128)}, f32[1,1024]{1,0:T(1,128)S(1)}, u32[]{:S(2)}) copy-start(f32[1,1024]{1,0:T(1,128)S(1)} %get-tuple-element.272) | copy-start | bytes 12292
  96.2 35.4 copy-start.82
  96.2 66.1 %copy-start.92 = (f32[1024]{0:T(1024)}, f32[1024]{0:T(1024)S(1)}, u32[]{:S(2)}) copy-start(f32[1024]{0:T(1024)S(1)} %fusion.80) | copy-start | bytes 12292
  132.4 38.0 collective-permute-start
  1026.9 6.2 copy-start.33
  1051.9 6.2 copy-start.31
  1082.9 6.2 copy-start.29
  1125.7 6.1 copy-start.65
  1504.6 69.2 %copy-start.102 = (f32[1,704]{1,0:T(1,128)S(1)}, f32[1,704]{1,0:T(1,128)}, u32[]{:S(2)}) copy-start(f32[1,704]{1,0:T(1,128)} %param.25) | copy-start | bytes 8452
  1590.6 337.3 %all-gather.17.cloned.1.call-start = ((), (), s32[]{:S(2)}) async-start(), calls=%async_computation.12 | async-start | bytes 7077888 | tf_op jit(solution)/shard_map/all_gather | solution.py:148
  1591.2 384.1 %all-gather.19.cloned.1.call-start = ((), (), s32[]{:S(2)}) async-start(), calls=%async_computation.13 | async-start | bytes 7077888 | tf_op jit(solution)/shard_map/all_gather | solution.py:149
  1592.0 466.3 %all-gather.23.cloned.1.call-start = ((), (), s32[]{:S(2)}) async-start(), calls=%async_computation.16 | async-start | bytes 5242880 | tf_op jit(solution)/shard_map/all_gather | solution.py:142
  1594.5 509.8 %all-gather.21.cloned.1.call-start = ((), (), s32[]{:S(2)}) async-start(), calls=%async_computation.14 | async-start | bytes 7077888 | tf_op jit(solution)/shard_map/all_gather | solution.py:150
  1595.2 295.8 %copy-start.73 = (f32[2048]{0:T(1024)S(1)}, f32[2048]{0:T(1024)}, u32[]{:S(2)}) copy-start(f32[2048]{0:T(1024)} %param.41) | copy-start | bytes 24580
  1595.2 839.5 %all-reduce.99.cloned.1.call-start = ((), (), s32[]{:S(2)}) async-start(), calls=%async_computation.17 | async-start | bytes 16777216 | tf_op jit(solution)/shard_map/psum | solution.py:227
  2122.7 10.0 copy-start.108
  2122.7 10.0 copy-start.103
  2143.7 1777.1 %reduce-scatter.8.cloned.1.call-start = ((), (), s32[]{:S(2)}) async-start(), calls=%async_computation.15 | async-start | bytes 10485760 | tf_op jit(solution)/shard_map/reduce_scatter | solution.py:207
  2352.8 1776.5 %all-reduce.101.cloned.1.call-start = ((), (), s32[]{:S(2)}) async-start(), calls=%async_computation.18 | async-start | bytes 16777216 | tf_op jit(solution)/shard_map/psum | solution.py:277
  2434.7 9.0 copy-start.12
  2443.7 6.3 copy-start.26
  2449.7 10.2 copy-start.13
  3182.2 6.2 copy-start.34
  3207.2 6.1 copy-start.32
  3238.1 6.2 copy-start.30
  3280.8 6.2 copy-start.64
  3762.9 30.2 copy-start.96
  3762.9 30.2 copy-start.5
  3762.9 30.2 copy-start.70
  3762.9 30.3 copy-start.72
  3762.9 30.3 copy-start.75
  3762.9 30.3 copy-start.77
  3793.2 8.6 copy-start.7
  3793.2 8.6 copy-start.9
  3810.6 7.3 copy-start.85
  3810.6 7.3 copy-start.87
  3810.6 7.3 copy-start.89
  3810.6 7.3 copy-start.91
  3819.2 10.5 collective-permute-start.2
  3839.6 351.1 %all-reduce.103.cloned.1.call-start = ((), (), s32[]{:S(2)}) async-start(), calls=%async_computation.25 | async-start | bytes 2883584 | tf_op jit(solution)/shard_map/psum | solution.py:289
  3845.1 408.1 %reduce-scatter.14.cloned.1.call-start = ((), (), s32[]{:S(2)}) async-start(), calls=%async_computation.21 | async-start | bytes 6488064 | tf_op jit(solution)/shard_map/reduce_scatter | solution.py:284
  3854.6 461.5 %reduce-scatter.12.cloned.1.call-start = ((), (), s32[]{:S(2)}) async-start(), calls=%async_computation.20 | async-start | bytes 6488064 | tf_op jit(solution)/shard_map/reduce_scatter | solution.py:283
  3863.3 516.2 %reduce-scatter.10.cloned.1.call-start = ((), (), s32[]{:S(2)}) async-start(), calls=%async_computation.19 | async-start | bytes 6488064 | tf_op jit(solution)/shard_map/reduce_scatter | solution.py:282
  3872.4 603.4 %reduce-scatter.16.cloned.1.call-start = ((), (), s32[]{:S(2)}) async-start(), calls=%async_computation.22 | async-start | bytes 14155776 | tf_op jit(solution)/shard_map/reduce_scatter | solution.py:285
  3885.0 687.2 %reduce-scatter.18.cloned.1.call-start = ((), (), s32[]{:S(2)}) async-start(), calls=%async_computation.23 | async-start | bytes 14155776 | tf_op jit(solution)/shard_map/reduce_scatter | solution.py:286
  3897.6 771.1 %reduce-scatter.20.cloned.1.call-start = ((), (), s32[]{:S(2)}) async-start(), calls=%async_computation.24 | async-start | bytes 14155776 | tf_op jit(solution)/shard_map/reduce_scatter | solution.py:287
  3912.2 8.5 copy-start.97
  3924.4 213.0 %copy-start.94 = (f32[2048]{0:T(1024)S(1)}, f32[2048]{0:T(1024)}, u32[]{:S(2)}) copy-start(f32[2048]{0:T(1024)} %get-tuple-element.134) | copy-start | bytes 24580
  3924.4 238.4 %copy-start.83 = (f32[1024]{0:T(1024)S(1)}, f32[1024]{0:T(1024)}, u32[]{:S(2)}) copy-start(f32[1024]{0:T(1024)} %copy-done.82) | copy-start | bytes 12292
  (67 other events, 199.5 us)
Sparse Core Ops, SparseCore 0:
  9.6 83.4 all-gather.8
  95.0 30.1 all-gather.10
  127.1 35.1 all-gather.12
  164.0 31.6 all-gather.14
  1590.8 290.8 all-reduce.96
  1883.4 44.5 all-gather.16
  1929.8 45.5 all-gather.18
  1977.5 80.7 all-gather.22
  2060.2 44.0 all-gather.20
  2143.8 290.8 all-reduce.98
  2437.0 143.4 reduce-scatter.7
  3839.7 289.5 all-reduce.100
  4133.1 57.5 all-reduce.102
  4195.0 58.2 reduce-scatter.13
  4257.1 59.0 reduce-scatter.11
  4320.4 59.0 reduce-scatter.9
  4383.4 92.3 reduce-scatter.15
  4479.7 92.3 reduce-scatter.17
  4576.2 92.3 reduce-scatter.19
where the time goes:
time: 4710 us; the launch traced here: 4680 us
  local copies, waits for them, and re-layouts  2710 us (58%)
  waiting for transfers between devices  1400 us (30%)
  other arithmetic  315 us (7%)
  matrix products  186 us (4%)
    slice x62, local copies, waits for them, and re-layouts, shards(): lax.associative_scan(affine, (shifted, hidden_grad), axis=1, reverse=True)  809 us
    slice x58, local copies, waits for them, and re-layouts, shards(): lax.associative_scan(affine, (retain, inflow), axis=1)  752 us
    pad x36, local copies, waits for them, and re-layouts, shards(): lax.associative_scan(affine, (retain, inflow), axis=1)  508 us
    pad x36, local copies, waits for them, and re-layouts, shards(): lax.associative_scan(affine, (shifted, hidden_grad), axis=1, reverse=True)  504 us
    psum x1, waiting for transfers between devices, shards(): branch = lax.psum(contract_last(gated, fetched[2]), 'rep')  286 us
    psum x1, waiting for transfers between devices, shards(): normed_grad = lax.psum(normed_terms, 'rep')  205 us
    reduce_scatter x1, waiting for transfers between devices, shards(): lax.psum_scatter(feed_down_grad, ('seq', 'row'), scatter_dimension=0, til...  96.5 us
    reduce_scatter x1, waiting for transfers between devices, shards(): lax.psum_scatter(feed_up_grad, ('seq', 'row'), scatter_dimension=0, tiled...  96.4 us
  transfers between devices with their start and end apart: 22, of which 18 were waited for; matrix products, arithmetic and copies ran while one was open for 67% of the time, Pallas kernels for 0%

commit v1 on v0

--- a/solution.py
+++ b/solution.py
@@ -196,7 +196,7 @@
     block_windows = conv_input[:, None, -edge_width:]
     gated_f, gated_back = jax.vjp(output_gate, hidden, gate_branch)
     gated = gated_f.astype(jnp.bfloat16)
-    branch = lax.psum(contract_last(gated, fetched[2]), "rep")
+    branch = jnp.sum(lax.all_gather(contract_last(gated, fetched[2]), "rep"), axis=0)
     middle = input_float + branch
     normed_mid_f, norm_two_back = jax.vjp(rms_norm, middle, feed_gain)
     normed_mid = normed_mid_f.astype(jnp.bfloat16)

time: 4710 us -> 4980 us (1.057)
  waiting for transfers between devices: 1400 us -> 1650 us
    all_gather x0 -> x1, waiting for transfers between devices: none -> 557 us  [shards(): lax.all_gather(contract_last(gated, fetched[2]), 'rep')]
    psum x1 -> x0, waiting for transfers between devices: 286 us -> none  [shards(): branch = lax.psum(contract_last(gated, fetched[2]), 'rep')]
  transfers between devices with their start and end apart: 22 -> 22, of which waited for: 18 -> 18; matrix products, arithmetic and copies ran while one was open for 67% -> 64% of each run, Pallas kernels for 0% -> 0%
where the time goes in v1:
time: 4980 us; the launch traced here: 4950 us
  local copies, waits for them, and re-layouts  2710 us (54%)
  waiting for transfers between devices  1650 us (33%)
  other arithmetic  331 us (7%)
  matrix products  185 us (4%)
    slice x62, local copies, waits for them, and re-layouts, shards(): lax.associative_scan(affine, (shifted, hidden_grad), axis=1, reverse=True)  809 us
    slice x58, local copies, waits for them, and re-layouts, shards(): lax.associative_scan(affine, (retain, inflow), axis=1)  752 us
    all_gather x1, waiting for transfers between devices, shards(): lax.all_gather(contract_last(gated, fetched[2]), 'rep')  557 us
    pad x36, local copies, waits for them, and re-layouts, shards(): lax.associative_scan(affine, (retain, inflow), axis=1)  508 us
    pad x36, local copies, waits for them, and re-layouts, shards(): lax.associative_scan(affine, (shifted, hidden_grad), axis=1, reverse=True)  504 us
    psum x1, waiting for transfers between devices, shards(): normed_grad = lax.psum(normed_terms, 'rep')  205 us
  transfers between devices with their start and end apart: 22, of which 18 were waited for; matrix products, arithmetic and copies ran while one was open for 64% of the time, Pallas kernels for 0%

profile of v1, /device:TPU:0, one launch (start us, length us, event | category | flops | bytes accessed | tf_op | source)
XLA Modules:
  0.0 4947.7 jit_solution(8598455003491217840)
XLA Ops:
  20.5 72.6 %all-gather.11.cloned.1.call-done = bf16[1,1024,2048]{2,1,0:T(8,128)(2,1)} async-done(((bf16[1,1024,512]{2,1,0:T(8,128)(2,1)}), bf16[1,1024,2048]{2,1,0:T(8,128)(2,1)}) %all-gather.11.cloned.1.call-update) | async-done | bytes 4194320 | tf_op jit(solution)/shard_map/all_gather | solution.py:141
  96.2 29.0 all-gather.13.cloned.1.call-done
  135.3 27.0 all-gather.15.cloned.1.call-done
  181.5 50.8 %slice.699 = f32[1,512,704]{1,2,0:T(8,128)} slice(f32[1,1024,704]{1,2,0:T(8,128)S(1)} %get-tuple-element.180), slice={[0:1:1], [1:1024:2], [0:704:1]} | slice | bytes 2883584 | tf_op jit(solution)/shard_map/slice | solution.py:185
  232.3 50.7 %slice.703 = f32[1,512,704]{1,2,0:T(8,128)} slice(f32[1,1024,704]{1,2,0:T(8,128)S(1)} %get-tuple-element.180), slice={[0:1:1], [0:1023:2], [0:704:1]} | slice | bytes 2883584 | tf_op jit(solution)/shard_map/slice | solution.py:185
  283.0 51.6 %slice.700 = f32[1,512,704]{1,2,0:T(8,128)} slice(f32[1,1024,704]{1,2,0:T(8,128)} %get-tuple-element.181), slice={[0:1:1], [0:1023:2], [0:704:1]} | slice | bytes 2883584 | tf_op jit(solution)/shard_map/slice | solution.py:185
  334.7 51.3 %slice.701 = f32[1,512,704]{1,2,0:T(8,128)} slice(f32[1,1024,704]{1,2,0:T(8,128)} %get-tuple-element.181), slice={[0:1:1], [1:1024:2], [0:704:1]} | slice | bytes 2883584 | tf_op jit(solution)/shard_map/slice | solution.py:185
  390.9 28.3 slice.706
  419.2 28.3 slice.707
  447.5 28.5 slice.705
  476.0 28.3 slice.709
  541.0 17.0 slice.711
  795.4 28.2 slice.704
  823.6 28.4 slice.769
  855.5 50.7 %slice.698 = f32[1,511,704]{1,2,0:T(8,128)} slice(f32[1,1024,704]{1,2,0:T(8,128)S(1)} %get-tuple-element.180), slice={[0:1:1], [2:1024:2], [0:704:1]} | slice | bytes 2877952 | tf_op jit(solution)/shard_map/slice | solution.py:185
  906.2 51.2 %slice.771 = f32[1,511,704]{1,2,0:T(8,128)} slice(f32[1,1024,704]{1,2,0:T(8,128)} %get-tuple-element.181), slice={[0:1:1], [2:1024:2], [0:704:1]} | slice | bytes 2877952 | tf_op jit(solution)/shard_map/slice | solution.py:185
  1198.9 28.7 pad.306
  1227.6 28.7 pad.307
  1256.3 28.9 pad.287
  1287.5 28.6 pad.286
  1326.0 57.0 %pad.308 = f32[1,1024,704]{1,2,0:T(8,128)} pad(f32[1,512,704]{1,2,0:T(8,128)} %pad_maximum_fusion.1, f32[]{:T(128)} %constant.20.clone.1), padding=0_0_0x0_1_1x0_0_0 | pad | bytes 4325380 | tf_op jit(solution)/shard_map/pad | solution.py:185
  1383.0 57.2 %pad.309 = f32[1,1024,704]{1,2,0:T(8,128)} pad(f32[1,512,704]{1,2,0:T(8,128)} %add.768, f32[]{:T(128)} %constant.20.clone.1), padding=0_0_0x1_0_1x0_0_0 | pad | bytes 4325380 | tf_op jit(solution)/shard_map/pad | solution.py:185
  1446.4 57.1 %pad.288 = f32[1,1024,704]{1,2,0:T(8,128)} pad(f32[1,512,704]{1,2,0:T(8,128)} %pad_maximum_fusion, f32[]{:T(128)} %constant.20.clone.1), padding=0_0_0x0_1_1x0_0_0 | pad | bytes 4325380 | tf_op jit(solution)/shard_map/pad | solution.py:185
  1503.4 57.3 %pad.289 = f32[1,1024,704]{1,2,0:T(8,128)} pad(f32[1,512,704]{1,2,0:T(8,128)} %add.757, f32[]{:T(128)} %constant.20.clone.1), padding=0_0_0x1_0_1x0_0_0 | pad | bytes 4325380 | tf_op jit(solution)/shard_map/pad | solution.py:185
  1594.0 556.9 %all-gather.27.cloned.1.call-done = f32[4096,2048]{1,0:T(8,128)} async-done(((f32[1024,2048]{1,0:T(8,128)}), f32[4096,2048]{1,0:T(8,128)}) %all-gather.27.cloned.1.call-update) | async-done | bytes 33554448 | tf_op jit(solution)/shard_map/all_gather | solution.py:199
  2150.9 16.9 reduce.13
  2208.1 35.7 all-gather.21.cloned.1.call-done
  2255.6 71.2 %all-gather.25.cloned.1.call-done = bf16[1,1024,2048]{2,1,0:T(8,128)(2,1)} async-done(((bf16[1,1024,512]{2,1,0:T(8,128)(2,1)}), bf16[1,1024,2048]{2,1,0:T(8,128)(2,1)}) %all-gather.25.cloned.1.call-update) | async-done | bytes 4194320 | tf_op jit(solution)/shard_map/all_gather | solution.py:142
  2326.8 46.0 all-gather.23.cloned.1.call-done
  2372.8 18.5 multiply_convert_fusion.2
  2414.5 51.4 %slice.798 = f32[1,512,704]{1,2,0:T(8,128)} slice(f32[1,1024,704]{1,2,0:T(8,128)} %concatenate.160), slice={[0:1:1], [0:1023:2], [0:704:1]} | slice | bytes 2883584 | tf_op jit(solution)/shard_map/slice | solution.py:238
  2465.9 51.3 %slice.805 = f32[1,512,704]{1,2,0:T(8,128)} slice(f32[1,1024,704]{1,2,0:T(8,128)} %concatenate.160), slice={[0:1:1], [1:1024:2], [0:704:1]} | slice | bytes 2883584 | tf_op jit(solution)/shard_map/slice | solution.py:238
  2517.2 51.3 %slice.796 = f32[1,511,704]{1,2,0:T(8,128)} slice(f32[1,1024,704]{1,2,0:T(8,128)} %concatenate.160), slice={[0:1:1], [1:1022:2], [0:704:1]} | slice | bytes 2877952 | tf_op jit(solution)/shard_map/slice | solution.py:238
  2621.1 81.8 %all-reduce.96.cloned.1.call-done = f32[1,1024,2048]{2,1,0:T(8,128)} async-done(((f32[1,1024,2048]{2,1,0:T(8,128)}), f32[1,1024,2048]{2,1,0:T(8,128)}) %all-reduce.96.cloned.1.call-update) | async-done | bytes 8388624 | tf_op jit(solution)/shard_map/psum | solution.py:227
  2730.6 51.3 %slice.800 = f32[1,512,704]{1,2,0:T(8,128)} slice(f32[1,1024,704]{1,2,0:T(8,128)} %multiply_bitcast_fusion), slice={[0:1:1], [1:1024:2], [0:704:1]} | slice | bytes 2883584 | tf_op jit(solution)/shard_map/slice | solution.py:238
  2781.9 51.4 %slice.802 = f32[1,512,704]{1,2,0:T(8,128)} slice(f32[1,1024,704]{1,2,0:T(8,128)} %multiply_bitcast_fusion), slice={[0:1:1], [0:1023:2], [0:704:1]} | slice | bytes 2883584 | tf_op jit(solution)/shard_map/slice | solution.py:238
  2864.8 28.3 slice.809
  2893.1 28.3 slice.810
  2921.4 28.3 slice.808
  2949.7 28.5 slice.812
  3031.8 17.2 slice.818
  3227.8 16.9 slice.813
  3265.0 28.2 slice.807
  3293.2 28.6 slice.872
  3325.3 51.3 %slice.874 = f32[1,511,704]{1,2,0:T(8,128)} slice(f32[1,1024,704]{1,2,0:T(8,128)} %multiply_bitcast_fusion), slice={[0:1:1], [1:1022:2], [0:704:1]} | slice | bytes 2877952 | tf_op jit(solution)/shard_map/slice | solution.py:238
  3623.2 28.9 pad.326
  3652.1 28.7 pad.327
  3684.0 57.2 %pad.329 = f32[1,1024,704]{1,2,0:T(8,128)} pad(f32[1,512,704]{1,2,0:T(8,128)} %add.810, f32[]{:T(128)} %constant.20.clone.1), padding=0_0_0x1_0_1x0_0_0 | pad | bytes 4325380 | tf_op jit(solution)/shard_map/pad | solution.py:238
  3743.5 28.7 pad.346
  3772.2 28.6 pad.347
  3822.9 57.1 %pad.328 = f32[1,1024,704]{1,2,0:T(8,128)} pad(f32[1,512,704]{1,2,0:T(8,128)} %pad_maximum_fusion.2, f32[]{:T(128)} %constant.20.clone.1), padding=0_0_0x0_1_1x0_0_0 | pad | bytes 4325380 | tf_op jit(solution)/shard_map/pad | solution.py:238
  3888.3 52.7 %pad.349 = f32[1,1024,704]{1,2,0:T(8,128)S(1)} pad(f32[1,512,704]{1,2,0:T(8,128)} %add.821, f32[]{:T(128)} %constant.20.clone.1), padding=0_0_0x1_0_1x0_0_0 | pad | bytes 4325380 | tf_op jit(solution)/shard_map/pad | solution.py:238
  3943.9 57.2 %pad.348 = f32[1,1024,704]{1,2,0:T(8,128)} pad(f32[1,512,704]{1,2,0:T(8,128)} %concatenate.178, f32[]{:T(128)} %constant.20.clone.1), padding=0_0_0x0_1_1x0_0_0 | pad | bytes 4325380 | tf_op jit(solution)/shard_map/pad | solution.py:238
  4005.1 25.7 rev.5
  4030.8 25.9 rev.4
  4192.5 204.7 %all-reduce.98.cloned.1.call-done = f32[1,1024,2048]{2,1,0:T(8,128)} async-done(((f32[1,1024,2048]{2,1,0:T(8,128)}), f32[1,1024,2048]{2,1,0:T(8,128)}) %all-reduce.98.cloned.1.call-update) | async-done | bytes 8388624 | tf_op jit(solution)/shard_map/psum | solution.py:277
  4405.4 25.4 all-reduce.90
  4435.2 23.5 all-reduce.100.cloned.1.call-done
  4458.7 62.5 %reduce-scatter.14.cloned.1.call-done = f32[256,704]{0,1:T(8,128)} async-done(((f32[2048,704]{0,1:T(8,128)}), f32[256,704]{0,1:T(8,128)}) %reduce-scatter.14.cloned.1.call-update) | async-done | bytes 720912 | tf_op jit(solution)/shard_map/reduce_scatter | solution.py:284
  4521.2 62.9 %reduce-scatter.12.cloned.1.call-done = f32[256,704]{0,1:T(8,128)} async-done(((f32[2048,704]{0,1:T(8,128)}), f32[256,704]{0,1:T(8,128)}) %reduce-scatter.12.cloned.1.call-update) | async-done | bytes 720912 | tf_op jit(solution)/shard_map/reduce_scatter | solution.py:283
  4584.1 63.3 %reduce-scatter.10.cloned.1.call-done = f32[256,704]{0,1:T(8,128)} async-done(((f32[2048,704]{0,1:T(8,128)}), f32[256,704]{0,1:T(8,128)}) %reduce-scatter.10.cloned.1.call-update) | async-done | bytes 720912 | tf_op jit(solution)/shard_map/reduce_scatter | solution.py:282
  4647.5 96.3 %reduce-scatter.16.cloned.1.call-done = f32[256,1536]{1,0:T(8,128)} async-done(((f32[2048,1536]{1,0:T(8,128)}), f32[256,1536]{1,0:T(8,128)}) %reduce-scatter.16.cloned.1.call-update) | async-done | bytes 1572880 | tf_op jit(solution)/shard_map/reduce_scatter | solution.py:285
  4743.8 96.4 %reduce-scatter.18.cloned.1.call-done = f32[256,1536]{1,0:T(8,128)} async-done(((f32[2048,1536]{1,0:T(8,128)}), f32[256,1536]{1,0:T(8,128)}) %reduce-scatter.18.cloned.1.call-update) | async-done | bytes 1572880 | tf_op jit(solution)/shard_map/reduce_scatter | solution.py:286
  4840.2 96.5 %reduce-scatter.20.cloned.1.call-done = f32[256,1536]{1,0:T(8,128)} async-done(((f32[2048,1536]{1,0:T(8,128)}), f32[256,1536]{1,0:T(8,128)}) %reduce-scatter.20.cloned.1.call-update) | async-done | bytes 1572880 | tf_op jit(solution)/shard_map/reduce_scatter | solution.py:287
  (643 shorter events, 1504.6 us)
Async XLA Ops:
  7.2 167.4 %copy-start = (bf16[4,176,176]{2,1,0:T(8,128)(2,1)S(1)}, bf16[4,176,176]{2,1,0:T(8,128)(2,1)}, u32[]{:S(2)}) copy-start(bf16[4,176,176]{2,1,0:T(8,128)(2,1)} %param.36) | copy-start | bytes 743428
  7.2 85.9 %all-gather.11.cloned.1.call-start = ((), (), s32[]{:S(2)}) async-start(), calls=%async_computation.7 | async-start | bytes 5242880 | tf_op jit(solution)/shard_map/all_gather | solution.py:141
  7.9 117.3 %copy-start.98 = (f32[2048]{0:T(1024)S(1)}, f32[2048]{0:T(1024)}, u32[]{:S(2)}) copy-start(f32[2048]{0:T(1024)} %param.40) | copy-start | bytes 24580
  8.0 117.3 %all-gather.13.cloned.1.call-start = ((), (), s32[]{:S(2)}) async-start(), calls=%async_computation.8 | async-start | bytes 3244032 | tf_op jit(solution)/shard_map/all_gather | solution.py:145
  8.7 153.6 %all-gather.15.cloned.1.call-start = ((), (), s32[]{:S(2)}) async-start(), calls=%async_computation.9 | async-start | bytes 3244032 | tf_op jit(solution)/shard_map/all_gather | solution.py:146
  9.4 1570.8 %all-gather.17.cloned.1.call-start = ((), (), s32[]{:S(2)}) async-start(), calls=%async_computation.10 | async-start | bytes 3244032 | tf_op jit(solution)/shard_map/all_gather | solution.py:147
  10.2 8.6 collective-permute-start.1
  15.1 2135.8 %all-gather.27.cloned.1.call-start = ((), (), s32[]{:S(2)}) async-start(), calls=%async_computation.24 | async-start | bytes 41943040 | tf_op jit(solution)/shard_map/all_gather | solution.py:199
  18.1 152.9 %copy-start.84 = (f32[704]{0:T(1024)}, f32[704]{0:T(1024)S(1)}, u32[]{:S(2)}) copy-start(f32[704]{0:T(1024)S(1)} %get-tuple-element.143) | copy-start | bytes 8452
  18.1 152.9 %copy-start.86 = (f32[704]{0:T(1024)}, f32[704]{0:T(1024)S(1)}, u32[]{:S(2)}) copy-start(f32[704]{0:T(1024)S(1)} %get-tuple-element.144) | copy-start | bytes 8452
  18.1 152.9 %copy-start.88 = (f32[704]{0:T(1024)}, f32[704]{0:T(1024)S(1)}, u32[]{:S(2)}) copy-start(f32[704]{0:T(1024)S(1)} %get-tuple-element.145) | copy-start | bytes 8452
  18.1 152.9 %copy-start.90 = (f32[704]{0:T(1024)}, f32[704]{0:T(1024)S(1)}, u32[]{:S(2)}) copy-start(f32[704]{0:T(1024)S(1)} %get-tuple-element.146) | copy-start | bytes 8452
  18.8 157.6 %copy-start.71 = (f32[704]{0:T(1024)}, f32[704]{0:T(1024)S(1)}, u32[]{:S(2)}) copy-start(f32[704]{0:T(1024)S(1)} %fusion.79) | copy-start | bytes 8452
  20.5 150.6 %copy-start.78 = (f32[1,1024]{1,0:T(1,128)}, f32[1,1024]{1,0:T(1,128)S(1)}, u32[]{:S(2)}) copy-start(f32[1,1024]{1,0:T(1,128)S(1)} %get-tuple-element.273) | copy-start | bytes 12292
  20.5 150.6 %copy-start.80 = (f32[1,1024]{1,0:T(1,128)}, f32[1,1024]{1,0:T(1,128)S(1)}, u32[]{:S(2)}) copy-start(f32[1,1024]{1,0:T(1,128)S(1)} %get-tuple-element.274) | copy-start | bytes 12292
  20.5 155.9 %copy-start.69 = (f32[1,1024]{1,0:T(1,128)}, f32[1,1024]{1,0:T(1,128)S(1)}, u32[]{:S(2)}) copy-start(f32[1,1024]{1,0:T(1,128)S(1)} %get-tuple-element.272) | copy-start | bytes 12292
  96.2 35.4 copy-start.82
  96.2 66.1 %copy-start.92 = (f32[1024]{0:T(1024)}, f32[1024]{0:T(1024)S(1)}, u32[]{:S(2)}) copy-start(f32[1024]{0:T(1024)S(1)} %fusion.80) | copy-start | bytes 12292
  132.3 37.8 collective-permute-start
  1026.2 6.2 copy-start.33
  1051.2 6.2 copy-start.31
  1082.0 6.2 copy-start.29
  1503.4 69.1 %copy-start.102 = (f32[1,704]{1,0:T(1,128)S(1)}, f32[1,704]{1,0:T(1,128)}, u32[]{:S(2)}) copy-start(f32[1,704]{1,0:T(1,128)} %param.25) | copy-start | bytes 8452
  1589.4 607.0 %all-gather.19.cloned.1.call-start = ((), (), s32[]{:S(2)}) async-start(), calls=%async_computation.11 | async-start | bytes 7077888 | tf_op jit(solution)/shard_map/all_gather | solution.py:148
  1589.9 653.9 %all-gather.21.cloned.1.call-start = ((), (), s32[]{:S(2)}) async-start(), calls=%async_computation.12 | async-start | bytes 7077888 | tf_op jit(solution)/shard_map/all_gather | solution.py:149
  1590.7 736.1 %all-gather.25.cloned.1.call-start = ((), (), s32[]{:S(2)}) async-start(), calls=%async_computation.15 | async-start | bytes 5242880 | tf_op jit(solution)/shard_map/all_gather | solution.py:142
  1593.2 779.6 %all-gather.23.cloned.1.call-start = ((), (), s32[]{:S(2)}) async-start(), calls=%async_computation.13 | async-start | bytes 7077888 | tf_op jit(solution)/shard_map/all_gather | solution.py:150
  1593.9 1108.9 %all-reduce.96.cloned.1.call-start = ((), (), s32[]{:S(2)}) async-start(), calls=%async_computation.16 | async-start | bytes 16777216 | tf_op jit(solution)/shard_map/psum | solution.py:227
  2167.9 9.6 copy-start.73
  2391.2 10.0 copy-start.108
  2391.2 10.0 copy-start.103
  2411.9 1777.0 %reduce-scatter.8.cloned.1.call-start = ((), (), s32[]{:S(2)}) async-start(), calls=%async_computation.14 | async-start | bytes 10485760 | tf_op jit(solution)/shard_map/reduce_scatter | solution.py:207
  2621.0 1776.2 %all-reduce.98.cloned.1.call-start = ((), (), s32[]{:S(2)}) async-start(), calls=%async_computation.17 | async-start | bytes 16777216 | tf_op jit(solution)/shard_map/psum | solution.py:277
  2702.9 9.0 copy-start.12
  2711.8 6.3 copy-start.26
  2717.9 10.2 copy-start.13
  3450.4 6.2 copy-start.34
  3506.2 6.2 copy-start.30
  3549.0 6.2 copy-start.64
  4030.8 30.3 copy-start.96
  4030.8 30.3 copy-start.5
  4030.8 30.3 copy-start.70
  4030.8 30.3 copy-start.72
  4030.8 30.3 copy-start.75
  4030.8 30.3 copy-start.77
  4061.1 8.6 copy-start.7
  4061.1 8.6 copy-start.9
  4078.6 7.3 copy-start.85
  4078.6 7.3 copy-start.87
  4078.6 7.3 copy-start.89
  4078.6 7.3 copy-start.91
  4087.2 10.5 collective-permute-start.2
  4091.9 6.2 copy-start.62
  4091.9 6.2 copy-start.104
  4107.6 351.1 %all-reduce.100.cloned.1.call-start = ((), (), s32[]{:S(2)}) async-start(), calls=%async_computation.25 | async-start | bytes 2883584 | tf_op jit(solution)/shard_map/psum | solution.py:289
  4113.1 408.1 %reduce-scatter.14.cloned.1.call-start = ((), (), s32[]{:S(2)}) async-start(), calls=%async_computation.20 | async-start | bytes 6488064 | tf_op jit(solution)/shard_map/reduce_scatter | solution.py:284
  4122.6 461.5 %reduce-scatter.12.cloned.1.call-start = ((), (), s32[]{:S(2)}) async-start(), calls=%async_computation.19 | async-start | bytes 6488064 | tf_op jit(solution)/shard_map/reduce_scatter | solution.py:283
  4131.3 516.1 %reduce-scatter.10.cloned.1.call-start = ((), (), s32[]{:S(2)}) async-start(), calls=%async_computation.18 | async-start | bytes 6488064 | tf_op jit(solution)/shard_map/reduce_scatter | solution.py:282
  4140.4 603.4 %reduce-scatter.16.cloned.1.call-start = ((), (), s32[]{:S(2)}) async-start(), calls=%async_computation.21 | async-start | bytes 14155776 | tf_op jit(solution)/shard_map/reduce_scatter | solution.py:285
  4153.0 687.2 %reduce-scatter.18.cloned.1.call-start = ((), (), s32[]{:S(2)}) async-start(), calls=%async_computation.22 | async-start | bytes 14155776 | tf_op jit(solution)/shard_map/reduce_scatter | solution.py:286
  4165.6 771.1 %reduce-scatter.20.cloned.1.call-start = ((), (), s32[]{:S(2)}) async-start(), calls=%async_computation.23 | async-start | bytes 14155776 | tf_op jit(solution)/shard_map/reduce_scatter | solution.py:287
  4180.3 8.5 copy-start.97
  4192.5 212.9 %copy-start.94 = (f32[2048]{0:T(1024)S(1)}, f32[2048]{0:T(1024)}, u32[]{:S(2)}) copy-start(f32[2048]{0:T(1024)} %get-tuple-element.134) | copy-start | bytes 24580
  4192.5 238.3 %copy-start.83 = (f32[1024]{0:T(1024)S(1)}, f32[1024]{0:T(1024)}, u32[]{:S(2)}) copy-start(f32[1024]{0:T(1024)} %copy-done.82) | copy-start | bytes 12292
  (67 other events, 199.7 us)
Sparse Core Ops, SparseCore 0:
  9.6 83.4 all-gather.10
  95.0 30.1 all-gather.12
  127.1 35.1 all-gather.14
  164.0 31.6 all-gather.16
  1589.5 561.3 all-gather.26
  2152.7 43.7 all-gather.18
  2198.3 45.5 all-gather.20
  2246.0 80.7 all-gather.24
  2328.7 44.0 all-gather.22
  2412.0 290.8 all-reduce.95
  2705.2 143.4 reduce-scatter.7
  4107.7 289.5 all-reduce.97
  4401.1 57.5 all-reduce.99
  4463.0 58.2 reduce-scatter.13
  4525.1 59.0 reduce-scatter.11
  4588.4 59.0 reduce-scatter.9
  4651.4 92.3 reduce-scatter.15
  4747.7 92.3 reduce-scatter.17
  4844.2 92.3 reduce-scatter.19
